TPU v7x, 32 devices: a whole 2x2x4 slice. The times are simulated.
32 devices in a mesh: row: 8 (over z, y), col: 4 (over x, core).
Axes of the slice: x: 2, y: 2, z: 4, core: 2. Of those that a mesh axis runs over, the one named last changes fastest.
Arguments:
- amplitudes: float32 [8, 8, 384, 384], P('row', 'col'), may hold values from -6 to 6
- exchange_ints: float32 [8, 8, 384, 384], P('row', 'col'), may hold values from -6 to 6
- virt_fock: float32 [384, 384], replicated, as said below
- intersection: float32 [384, 384], replicated, as said below
- occ_fock: float32 [8, 8], replicated, may hold values from -1.5 to 0.3, as said below
- virt_energy: float32 [384], replicated, may hold values from 1 to 3
- fock_tiles: int32 [3, 3], replicated, may hold values from 0 to 1, as said below
- intersection_tiles: int32 [3, 3], replicated, may hold values from 0 to 1, as said below
- occ_pattern: int32 [8, 8], replicated, may hold values from 0 to 1, as said below
- pair_domain: int32 [8, 8, 3], P('row', 'col'), may hold values 0 or 1
Outputs:
- new_amplitudes: float32 [8, 8, 384, 384], P('row', 'col')
Inputs may be any that keep to these rules, and one draw needn't show every extreme that they name: `virt_fock`: symmetric. `intersection`: symmetric. `occ_fock`: diagonal entries between -1.5 and -0.3, the others between -0.3 and 0.3. `fock_tiles`: symmetric, every diagonal tile 1, some off-diagonal tile 0. `intersection_tiles`: symmetric, every diagonal tile 1, some off-diagonal tile 0. `occ_pattern`: 1 on the diagonal, 0 where the two orbitals lie more than 1 apart in index.
All inputs are finite; a program needn't handle non-finite values. No bound on the sum of `pair_domain` on one device may be relied on, other than what follows from the above.
Results may differ from a plain program's by a relative error of at most 0.0001.
Values sent between devices are 32-bit elements; how exact they have to be, the bound alone decides.
No kernel may reach another device: no remote copies, remote signals or barrier semaphores. Data moves between devices by JAX's collectives and lax.ppermute only.
A program may use at most 64 MiB of HBM per device.

v0:
```python
import functools

import jax
import jax.numpy as jnp
import numpy as np
from jax import lax
from jax.experimental import pallas as pl
from jax.experimental.pallas import tpu as pltpu
from jax.sharding import PartitionSpec as P

ITERS = 2
AXES = ("row", "col")
PAD = 8


def slot_of(i, j):
    if i == j:
        return i % 2
    return (i + j + (i > j)) % 2


def list_units(count):
    units = [((i, j), (j, i)) for i in range(count) for j in range(i + 1, count)]
    units += [((i, i), (i + 1, i + 1)) for i in range(0, count, 2)]
    return [tuple(sorted(unit, key=lambda block: slot_of(*block))) for unit in units]


def first_hosts(units, cols):
    hosts = []
    for unit in units:
        i, j = min(unit[0], unit[1])
        if unit[0][0] == unit[0][1]:
            hosts.append((i + 1) * cols + i // 2)
        elif i // 2 == j // 2:
            hosts.append(i * cols + j // 2)
        elif (i + j) % 2 == 0:
            hosts.append(i * cols + j // 2)
        else:
            hosts.append(j * cols + i // 2)
    return hosts


def chip_coords(mesh, cols):
    devices = list(mesh.devices.flat)
    if all(getattr(d, "coords", None) is not None for d in devices):
        return [tuple(d.coords) for d in devices]
    return [(k % cols // 2, k // cols, 0) for k in range(len(devices))]


def route_matrix(chips):
    index = {chip: k for k, chip in enumerate(chips)}
    links = {}
    rows = []
    for a in chips:
        for b in chips:
            here, path = list(a), []
            for axis in (2, 0, 1):
                while here[axis] != b[axis]:
                    there = list(here)
                    there[axis] += 1 if b[axis] > here[axis] else -1
                    if tuple(there) not in index:
                        return None
                    path.append(links.setdefault((tuple(here), tuple(there)), len(links)))
                    here = there
            rows.append(path)
    matrix = np.zeros((len(rows), max(1, len(links))), np.float32)
    for k, path in enumerate(rows):
        matrix[k, path] = 1.0
    return matrix


def choose_hosts(mesh, units, count, cols):
    hosts = first_hosts(units, cols)
    coords = chip_coords(mesh, cols)
    chips = sorted(set(coords))
    if len(chips) > 32:
        return hosts
    routes = route_matrix(chips)
    if routes is None:
        return hosts
    number = len(chips)
    chip_of_device = np.array([chips.index(c) for c in coords])
    block_unit = np.zeros((count, count), np.int64)
    for u, unit in enumerate(units):
        for i, j in unit:
            block_unit[i, j] = u
    owner = np.array([[chip_of_device[i * cols + j // 2] for j in range(count)] for i in range(count)])
    up = np.concatenate([block_unit[:-1].ravel(), block_unit[1:].ravel()])
    down = np.concatenate([block_unit[1:].ravel(), block_unit[:-1].ravel()])
    flat_unit, flat_owner = block_unit.ravel(), owner.ravel()
    pairs = number * number

    chains, steps = 32, 10000
    draw = np.random.RandomState(78)
    offset = (np.arange(chains) * 3 * pairs)[:, None]

    def price(hosts):
        at = chip_of_device[hosts]
        here = at[:, flat_unit]
        keys = [flat_owner * number + here, pairs + here * number + flat_owner, 2 * pairs + at[:, up] * number + at[:, down]]
        keys = np.concatenate(keys, axis=1) + offset
        flows = np.bincount(keys.ravel(), minlength=3 * pairs * chains).astype(np.float32)
        loads = (flows.reshape(-1, pairs) @ routes).reshape(chains, 3, -1)
        there, back, halo = loads[:, 0], loads[:, 1], loads[:, 2]
        peak = there.max(1) + back.max(1) + 2.0 * halo.max(1) + 0.3 * (halo + 2.0 * there).max(1)
        return peak + 0.01 * (loads * loads).sum((1, 2))

    current = np.tile(np.array(hosts), (chains, 1))
    cost = price(current)
    best_cost, best = cost.min(), current[cost.argmin()].copy()
    each = np.arange(chains)
    for step in range(steps):
        heat = 1.5 * 0.02 ** (step / steps)
        a, b = draw.randint(len(units), size=(2, chains))
        trial = current.copy()
        trial[each, a], trial[each, b] = current[each, b], current[each, a]
        trial_cost = price(trial)
        take = (trial_cost <= cost) | (np.exp(np.minimum(0.0, (cost - trial_cost) / heat)) > draw.random_sample(chains))
        current[take], cost[take] = trial[take], trial_cost[take]
        if cost.min() < best_cost:
            best_cost, best = cost.min(), current[cost.argmin()].copy()
    return [int(h) for h in best]


def two_colours(edges):
    by_end = {}
    for k, (source, target) in enumerate(edges):
        by_end.setdefault(("s", source), []).append(k)
        by_end.setdefault(("t", target), []).append(k)
    colour = {}
    for start in range(len(edges)):
        stack = [] if start in colour else [start]
        if stack:
            colour[start] = 0
        while stack:
            k = stack.pop()
            for end in (("s", edges[k][0]), ("t", edges[k][1])):
                for other in by_end[end]:
                    if other not in colour:
                        colour[other] = 1 - colour[k]
                        stack.append(other)
    assert all(len({colour[k] for k in ks}) == len(ks) for ks in by_end.values())
    return [colour[k] for k in range(len(edges))]


def make_plan(mesh, count):
    rows, cols = mesh.shape["row"], mesh.shape["col"]
    assert count == rows and count == 2 * cols
    units = list_units(count)
    hosts = choose_hosts(mesh, units, count, cols)
    host = {}
    for unit, device in zip(units, hosts):
        for block in unit:
            host[block] = device
    devices = rows * cols
    table = np.zeros((devices, 16), np.int32)
    gather = [[], []]
    for unit, device in zip(units, hosts):
        for s, (i, j) in enumerate(unit):
            owner = i * cols + j // 2
            gather[s].append((owner, device))
            table[device, 2 * s : 2 * s + 2] = (i, j)
        table[device, 4] = int(unit[0][0] == unit[0][1])
    table[:, 6::2] = -1
    halo = []
    for s in range(2):
        moves = [
            (i, j, k)
            for i in range(count)
            for j in range(count)
            if slot_of(i, j) == s
            for k in (i - 1, i + 1)
            if 0 <= k < count
        ]
        edges = [(host[i, j], host[k, j]) for i, j, k in moves]
        colours = two_colours(edges)
        for colour in range(2):
            number = len(halo)
            halo.append([e for e, c in zip(edges, colours) if c == colour])
            for (i, j, k), (_, target), c in zip(moves, edges, colours):
                if c == colour:
                    place = 5 + 4 * slot_of(k, j)
                    place += 2 * (table[target, place + 1] >= 0)
                    table[target, place : place + 2] = (number, i)
    return table, gather, halo


DOT = functools.partial(lax.dot_general, preferred_element_type=jnp.float32)
MATMUL = (((1,), (0,)), ((), ()))


def split(value):
    high = value.astype(jnp.bfloat16)
    low = (value - high.astype(jnp.float32)).astype(jnp.bfloat16)
    return high, low


def constants_kernel(fock_tiles, over_tiles, fock, over, fock_left, over_left, over_right):
    size = fock.shape[0]
    tiles = fock_tiles.shape[0]
    tile = size // tiles
    for a in range(tiles):
        for b in range(tiles):
            rows, cols = pl.ds(a * tile, tile), pl.ds(b * tile, tile)
            high, low = split(fock[rows, cols] * fock_tiles[a, b].astype(jnp.float32))
            for part, value in enumerate((high, high, low)):
                fock_left[rows, pl.ds(part * size + b * tile, tile)] = value
            high, low = split(over[rows, cols] * over_tiles[a, b].astype(jnp.float32))
            for part, value in enumerate((high, high, low)):
                over_left[rows, pl.ds(part * size + b * tile, tile)] = value
            for part, value in enumerate((high, high, low)):
                over_right[pl.ds(part * size + a * tile, tile), cols] = value


PIECE = 16


def pieces(size, begin=0):
    return [pl.ds(begin + n * PIECE, PIECE) for n in range(size // PIECE)]


def three_pass(wide, tall, left):
    size = min(wide.shape[1], tall.shape[0]) // 2
    first = DOT(wide[:, pl.ds(0, 2 * size)], tall[pl.ds(0, 2 * size), :], MATMUL)
    if left:
        return first + DOT(wide[:, pl.ds(2 * size, size)], tall[pl.ds(0, size), :], MATMUL)
    return first + DOT(wide[:, pl.ds(0, size)], tall[pl.ds(2 * size, size), :], MATMUL)


def first_slot():
    i, j = lax.axis_index("row"), lax.axis_index("col") * 2
    return (i + (i > j).astype(jnp.int32)) % 2


def pick_kernel(blocks, out, sem, *, second):
    slot = 1 - first_slot() if second else first_slot()
    copy = pltpu.make_async_copy(blocks.at[slot], out, sem)
    copy.start()
    copy.wait()


def pick_masked_kernel(domain, blocks, out0, out1, sems):
    size = blocks.shape[1]
    tiles = domain.shape[1]
    tile = size // tiles
    first = first_slot()
    slots, outs = (first, 1 - first), (out0, out1)
    body = pl.ds(0, size)
    copies = [pltpu.make_async_copy(blocks.at[slots[s]], outs[s].at[body], sems.at[s]) for s in range(2)]
    for copy in copies:
        copy.start()
    top = lax.broadcasted_iota(jnp.int32, (PAD, tile), 0) == 0
    for s in range(2):
        for t in range(tiles):
            value = domain[slots[s], t].astype(jnp.float32)
            outs[s][pl.ds(size, PAD), pl.ds(t * tile, tile)] = jnp.where(top, value, 0.0)
    for copy in copies:
        copy.wait()


def couple(occ, pattern, i, k):
    return occ[i, k] * pattern[i, k].astype(jnp.float32)


def own_kernel(table, occ, pattern, x0, x1, fock_left, over_left, out, stack):
    size = x0.shape[0]
    for s, x in enumerate((x0, x1)):
        for part in pieces(size):
            high, low = split(x[part, :])
            stack[part, pl.ds(s * size, size)] = high
            stack[pl.ds(size + part.start, PIECE), pl.ds(s * size, size)] = low
    out[...] = three_pass(fock_left, stack, True)
    over_x = three_pass(over_left, stack, True)
    for s in range(2):
        i, cols = table[2 * s], pl.ds(s * size, size)
        out[:, cols] = out[:, cols] - couple(occ, pattern, i, i) * over_x[:, s * size : (s + 1) * size]


def scale_kernel(table, occ, e_col, e_row, scale):
    for s in range(2):
        i, j = table[2 * s], table[2 * s + 1]
        scale[s] = 1.0 / (e_col[...] + e_row[...] - occ[i, i] - occ[j, j])


def update_kernel(
    table, occ, pattern, x0, x1, r0, r1, r2, r3, own, over_left, over_right, scale, k0, k1,
    y0, y1, stack, left, half, g,
):
    size = x0.shape[0]
    halo, x, k, y = (r0, r1, r2, r3), (x0, x1), (k0, k1), (y0, y1)
    coefs = []
    for s in range(2):
        factors = [couple(occ, pattern, table[2 * s], jnp.maximum(table[place + 1], 0)) for place in (5 + 4 * s, 7 + 4 * s)]
        coefs.append([0.0] * len(halo))
        for place, factor in zip((5 + 4 * s, 7 + 4 * s), factors):
            for number in range(len(halo)):
                here = (table[place] == number) & (table[place + 1] >= 0)
                coefs[s][number] += jnp.where(here, factor, 0.0)
    for part in pieces(size):
        for s in range(2):
            value = 0.0
            for number, r in enumerate(halo):
                value += coefs[s][number] * r[part, :]
            high, low = split(value)
            stack[part, pl.ds(s * size, size)] = high
            stack[pl.ds(size + part.start, PIECE), pl.ds(s * size, size)] = low
    half[...] = three_pass(over_left, stack, True)
    for s in range(2):
        for part in pieces(size):
            cols = pl.ds(s * size, size)
            high, low = split(own[part, cols] - half[part, cols])
            rows_s = pl.ds(s * size + part.start, PIECE)
            left[rows_s, pl.ds(0, size)] = high
            left[rows_s, pl.ds(size, size)] = low
    g[...] = three_pass(left, over_right, False)
    other = 1 - table[4]
    tile = min(size, 128)
    for s in range(2):
        base = (other if s == 0 else 1 - other) * size
        mask = k[s][pl.ds(size, PAD), :]
        for a in range(0, size, tile):
            mask_rows = DOT(mask[:, a : a + tile], mask, (((0,), (0,)), ((), ())))
            for b in range(0, size, tile):
                rows_a, cols_b = pl.ds(a, tile), pl.ds(b, tile)
                mirror = g[pl.ds(pl.multiple_of(base + b, tile), tile), rows_a].T
                total = k[s][rows_a, cols_b] + g[pl.ds(s * size + a, tile), cols_b] + mirror
                factor = mask_rows[:, b : b + tile] * scale[s, rows_a, cols_b]
                y[s][rows_a, cols_b] = x[s][rows_a, cols_b] - factor * total


SMEM = functools.partial(pl.BlockSpec, memory_space=pltpu.SMEM)
VMEM = functools.partial(pl.BlockSpec, memory_space=pltpu.VMEM)
ANY = functools.partial(pl.BlockSpec, memory_space=pl.ANY)
LIMIT = pltpu.CompilerParams(vmem_limit_bytes=24 * 2**20)


def constants(fock_tiles, over_tiles, fock, over):
    size = fock.shape[0]
    wide = pltpu.VMEM((size, 3 * size), jnp.bfloat16)
    return pl.pallas_call(
        constants_kernel,
        compiler_params=LIMIT,
        in_specs=[SMEM(), SMEM(), VMEM(), VMEM()],
        out_specs=[VMEM()] * 3,
        out_shape=[wide, wide, pltpu.VMEM((3 * size, size), jnp.bfloat16)],
    )(fock_tiles, over_tiles, fock, over)


def pick(blocks, second):
    return pl.pallas_call(
        functools.partial(pick_kernel, second=second),
        compiler_params=LIMIT,
        in_specs=[ANY()],
        out_specs=VMEM(),
        out_shape=pltpu.VMEM(blocks.shape[1:], blocks.dtype),
        scratch_shapes=[pltpu.SemaphoreType.DMA],
    )(blocks)


def pick_masked(blocks, domain):
    size = blocks.shape[1]
    block = pltpu.VMEM((size + PAD, size), blocks.dtype)
    return pl.pallas_call(
        pick_masked_kernel,
        compiler_params=LIMIT,
        in_specs=[SMEM(), ANY()],
        out_specs=[VMEM()] * 2,
        out_shape=[block] * 2,
        scratch_shapes=[pltpu.SemaphoreType.DMA((2,))],
    )(domain, blocks)


def own_part(table, occ, pattern, x, fock_left, over_left):
    size = x[0].shape[0]
    return pl.pallas_call(
        own_kernel,
        compiler_params=LIMIT,
        in_specs=[SMEM()] * 3 + [VMEM()] * 4,
        out_specs=VMEM(),
        out_shape=pltpu.VMEM((size, 2 * size), jnp.float32),
        scratch_shapes=[pltpu.VMEM((2 * size, 2 * size), jnp.bfloat16)],
    )(table, occ, pattern, *x, fock_left, over_left)


def scale_part(table, occ, e_col, e_row):
    size = e_col.shape[0]
    return pl.pallas_call(
        scale_kernel,
        compiler_params=LIMIT,
        in_specs=[SMEM()] * 2 + [VMEM()] * 2,
        out_specs=VMEM(),
        out_shape=pltpu.VMEM((2, size, size), jnp.float32),
    )(table, occ, e_col, e_row)


def update(table, occ, pattern, x, halo, own, over_left, over_right, scale, k):
    size = x[0].shape[0]
    block = pltpu.VMEM((size, size), jnp.float32)
    return pl.pallas_call(
        update_kernel,
        compiler_params=LIMIT,
        in_specs=[SMEM()] * 3 + [VMEM()] * 12,
        out_specs=[VMEM()] * 2,
        out_shape=[block, block],
        scratch_shapes=[
            pltpu.VMEM((2 * size, 2 * size), jnp.bfloat16),
            pltpu.VMEM((2 * size, 2 * size), jnp.bfloat16),
            pltpu.VMEM((size, 2 * size), jnp.float32),
            pltpu.VMEM((2 * size, size), jnp.float32),
        ],
    )(table, occ, pattern, *x, *halo, own, over_left, over_right, scale, *k)


def send(value, moves):
    value = lax.ppermute(value, AXES, moves)
    return pltpu.with_memory_space_constraint(value, pltpu.VMEM)


def solution(mesh):
    def shards(amplitudes, exchange_ints, fock, over, occ, energy, fock_tiles, over_tiles, pattern, domain):
        count = occ.shape[0]
        assert amplitudes.shape[:2] == (1, 2)
        table, gather, halo = make_plan(mesh, count)
        device = lax.axis_index("row") * mesh.shape["col"] + lax.axis_index("col")
        table = lax.dynamic_index_in_dim(jnp.asarray(table), device, keepdims=False)
        straight = first_slot() == 0

        def by_slot(a, b):
            return jnp.where(straight, a, b), jnp.where(straight, b, a)

        own_x = [pick(amplitudes[0], False)]
        blocks, own_x[0] = lax.optimization_barrier((amplitudes, own_x[0]))
        own_x.append(pick(blocks[0], True))
        x = [send(own_x[n], gather[n]) for n in range(2)]
        integrals, own_x = lax.optimization_barrier((exchange_ints, own_x))
        own_k = pick_masked(integrals[0], domain[0])
        k = [send(own_k[n], gather[n]) for n in range(2)]
        scale = scale_part(table, occ, energy[:, None], energy[None, :])
        ready = (constants(fock_tiles, over_tiles, fock, over), scale, table)
        x[0], ready = lax.optimization_barrier((x[0], ready))
        (fock_left, over_left, over_right), scale, table = ready
        for _ in range(ITERS):
            nearby = [send(x[n // 2], moves) for n, moves in enumerate(halo)]
            own = own_part(table, occ, pattern, x, fock_left, over_left)
            x = update(table, occ, pattern, x, nearby, own, over_left, over_right, scale, k)
        back = [
            lax.ppermute(value, AXES, [(target, source) for source, target in moves])
            for value, moves in zip(x, gather)
        ]
        return jnp.stack(by_slot(*back))[None]

    blocks = P("row", "col", None, None)
    in_specs = (blocks, blocks, P(), P(), P(), P(), P(), P(), P(), P("row", "col", None))
    return jax.shard_map(shards, mesh=mesh, in_specs=in_specs, out_specs=blocks, check_vma=False)
```

profile of v0, /device:TPU:0, one launch (start us, length us, event | category | flops | bytes accessed | tf_op | source)
XLA Modules:
  0.0 138.7 jit_solution(12353861893255574395)
XLA Ops:
  0.0 1.3 copy-done
  1.3 1.0 shard_map.109
  2.4 1.1 copy-done.1
  3.5 1.9 %shard_map.114 = (f32[392,384]{1,0:T(8,128)}, f32[392,384]{1,0:T(8,128)}) custom-call(s32[2,3]{1,0:T(2,128)S(1)} %bitcast.15, f32[2,384,384]{2,1,0:T(8,128)S(1)} %bitcast.14), custom_call_target="tpu_custom_call" | custom-call | tf_op jit(solution)/shard_map/pallas_call | solution.py:363
  5.4 4.9 %collective-permute-start.6 = (f32[392,384]{1,0:T(8,128)}, f32[392,384]{1,0:T(8,128)S(1)}, u32[]{:S(2)}, u32[]{:S(2)}) collective-permute-start(f32[392,384]{1,0:T(8,128)} %get-tuple-element.35), channel_id=1, source_target_pairs={{4,5},{1,1},{12,7},{2,6},{20,3},{3,10},{28,15},{8,13},{5,14},{16,2... | collective-permute-start | bytes 1806344 | tf_op jit(solution)/shard_map/ppermute | solution.py:415
  10.3 1.9 %collective-permute-start = (f32[384,384]{1,0:T(8,128)}, f32[384,384]{1,0:T(8,128)S(1)}, u32[]{:S(2)}, u32[]{:S(2)}) collective-permute-start(f32[384,384]{1,0:T(8,128)} %shard_map.109), channel_id=1, source_target_pairs={{4,5},{1,1},{12,7},{2,6},{20,3},{3,10},{28,15},{8,13},{5,14},{16,2... | collective-permute-start | bytes 1769480 | tf_op jit(solution)/shard_map/ppermute | solution.py:415
  12.2 5.7 %collective-permute-start.1 = (f32[384,384]{1,0:T(8,128)S(1)}, f32[384,384]{1,0:T(8,128)S(1)}, u32[]{:S(2)}, u32[]{:S(2)}) collective-permute-start(f32[384,384]{1,0:T(8,128)S(1)} %shard_map.112), channel_id=1, source_target_pairs={{0,5},{8,1},{1,7},{16,6},{2,3},{24,10},{3,15},{5,13},{12,14},{6,2}... | collective-permute-start | bytes 1769480 | tf_op jit(solution)/shard_map/ppermute | solution.py:415
  17.9 1.9 %collective-permute-start.7 = (f32[392,384]{1,0:T(8,128)}, f32[392,384]{1,0:T(8,128)S(1)}, u32[]{:S(2)}, u32[]{:S(2)}) collective-permute-start(f32[392,384]{1,0:T(8,128)} %get-tuple-element.36), channel_id=1, source_target_pairs={{0,5},{8,1},{1,7},{16,6},{2,3},{24,10},{3,15},{5,13},{12,14},{6,2}... | collective-permute-start | bytes 1806344 | tf_op jit(solution)/shard_map/ppermute | solution.py:415
  20.8 0.8 shard_map.111.scale
  21.7 0.9 shard_map.110
  22.6 3.1 %collective-permute-done.x0 = f32[384,384]{1,0:T(8,128)S(1)} collective-permute-done((f32[384,384]{1,0:T(8,128)}, f32[384,384]{1,0:T(8,128)S(1)}, u32[]{:S(2)}, u32[]{:S(2)}) %collective-permute-start) | collective-permute-done | bytes 589856 | tf_op jit(solution)/shard_map/ppermute | solution.py:415
  25.7 2.8 %collective-permute-start.3 = (f32[384,384]{1,0:T(8,128)S(1)}, f32[384,384]{1,0:T(8,128)S(1)}, u32[]{:S(2)}, u32[]{:S(2)}) collective-permute-start(f32[384,384]{1,0:T(8,128)S(1)} %collective-permute-done.x0), channel_id=1, source_target_pairs={{5,1},{14,11},{0,17},{12,28},{13,4},{9,13},{19,2},{16,8},{7,6},{11... | collective-permute-start | bytes 1769480 | tf_op jit(solution)/shard_map/ppermute | solution.py:415
  28.5 37.2 %collective-permute-done.1.x1 = f32[384,384]{1,0:T(8,128)S(1)} collective-permute-done((f32[384,384]{1,0:T(8,128)S(1)}, f32[384,384]{1,0:T(8,128)S(1)}, u32[]{:S(2)}, u32[]{:S(2)}) %collective-permute-start.1) | collective-permute-done | bytes 589856 | tf_op jit(solution)/shard_map/ppermute | solution.py:415
  65.7 1.9 %collective-permute-start.5 = (f32[384,384]{1,0:T(8,128)S(1)}, f32[384,384]{1,0:T(8,128)S(1)}, u32[]{:S(2)}, u32[]{:S(2)}) collective-permute-start(f32[384,384]{1,0:T(8,128)S(1)} %collective-permute-done.1.x1), channel_id=1, source_target_pairs={{4,13},{13,9},{2,19},{8,16},{1,5},{11,14},{17,0},{28,12},{14,2},{9... | collective-permute-start | bytes 1769480 | tf_op jit(solution)/shard_map/ppermute | solution.py:415
  67.7 1.7 %collective-permute-start.2 = (f32[384,384]{1,0:T(8,128)S(1)}, f32[384,384]{1,0:T(8,128)S(1)}, u32[]{:S(2)}, u32[]{:S(2)}) collective-permute-start(f32[384,384]{1,0:T(8,128)S(1)} %collective-permute-done.x0), channel_id=1, source_target_pairs={{4,5},{1,13},{6,2},{10,8},{5,4},{14,7},{0,3},{12,15},{13,14},{9,11... | collective-permute-start | bytes 1769480 | tf_op jit(solution)/shard_map/ppermute | solution.py:415
  69.5 2.5 %shard_map.113.own = f32[384,768]{1,0:T(8,128)S(1)} custom-call(s32[16]{0:T(128)S(1)} %dynamic-slice_bitcast_fusion.table, f32[8,8]{1,0:T(8,128)S(1)} %copy-done.4, s32[8,8]{1,0:T(8,128)S(1)} %copy-done.5, f32[384,384]{1,0:T(8,128)S(1)} %collective-permute-done.x0, f32[384,384]{1,0:T(8,128)S(1)} %collective-permute-done.1.x1, ...), custom_call_target="tpu_custom_call" | custom-call | tf_op jit(solution)/shard_map/pallas_call | solution.py:375
  72.0 1.7 %collective-permute-done.7.k1 = f32[392,384]{1,0:T(8,128)S(1)} collective-permute-done((f32[392,384]{1,0:T(8,128)}, f32[392,384]{1,0:T(8,128)S(1)}, u32[]{:S(2)}, u32[]{:S(2)}) %collective-permute-start.7) | collective-permute-done | bytes 602144 | tf_op jit(solution)/shard_map/ppermute | solution.py:415
  73.7 7.1 %collective-permute-done.5.r3 = f32[384,384]{1,0:T(8,128)S(1)} collective-permute-done((f32[384,384]{1,0:T(8,128)S(1)}, f32[384,384]{1,0:T(8,128)S(1)}, u32[]{:S(2)}, u32[]{:S(2)}) %collective-permute-start.5) | collective-permute-done | bytes 589856 | tf_op jit(solution)/shard_map/ppermute | solution.py:415
  80.8 1.9 %collective-permute-done.4.r2 = f32[384,384]{1,0:T(8,128)S(1)} collective-permute-done((f32[384,384]{1,0:T(8,128)S(1)}, f32[384,384]{1,0:T(8,128)S(1)}, u32[]{:S(2)}, u32[]{:S(2)}) %collective-permute-start.4) | collective-permute-done | bytes 589856 | tf_op jit(solution)/shard_map/ppermute | solution.py:415
  83.4 3.9 %shard_map.115 = (f32[384,384]{1,0:T(8,128)S(1)}, f32[384,384]{1,0:T(8,128)S(1)}) custom-call(s32[16]{0:T(128)S(1)} %dynamic-slice_bitcast_fusion.table, f32[8,8]{1,0:T(8,128)S(1)} %copy-done.4, s32[8,8]{1,0:T(8,128)S(1)} %copy-done.5, f32[384,384]{1,0:T(8,128)S(1)} %collective-permute-done.x0, f32[384,384]{1,0:T(8,128)S(1)} %collective-permute-done.1.x1, ...), custom_call_target="tpu_custom_call" | custom-call | tf_op jit(solution)/shard_map/pallas_call | solution.py:399
  87.3 1.9 %collective-permute-start.9 = (f32[384,384]{1,0:T(8,128)S(1)}, f32[384,384]{1,0:T(8,128)S(1)}, u32[]{:S(2)}, u32[]{:S(2)}) collective-permute-start(f32[384,384]{1,0:T(8,128)S(1)} %get-tuple-element.37.x0), channel_id=1, source_target_pairs={{5,1},{14,11},{0,17},{12,28},{13,4},{9,13},{19,2},{16,8},{7,6},{11... | collective-permute-start | bytes 1769480 | tf_op jit(solution)/shard_map/ppermute | solution.py:415
  89.3 3.9 %collective-permute-start.11 = (f32[384,384]{1,0:T(8,128)S(1)}, f32[384,384]{1,0:T(8,128)S(1)}, u32[]{:S(2)}, u32[]{:S(2)}) collective-permute-start(f32[384,384]{1,0:T(8,128)S(1)} %get-tuple-element.38.x1), channel_id=1, source_target_pairs={{4,13},{13,9},{2,19},{8,16},{1,5},{11,14},{17,0},{28,12},{14,2},{9... | collective-permute-start | bytes 1769480 | tf_op jit(solution)/shard_map/ppermute | solution.py:415
  93.2 1.7 %collective-permute-start.10 = (f32[384,384]{1,0:T(8,128)S(1)}, f32[384,384]{1,0:T(8,128)S(1)}, u32[]{:S(2)}, u32[]{:S(2)}) collective-permute-start(f32[384,384]{1,0:T(8,128)S(1)} %get-tuple-element.38.x1), channel_id=1, source_target_pairs={{5,4},{7,14},{3,0},{15,12},{4,5},{13,1},{2,6},{8,10},{1,7},{11,9},... | collective-permute-start | bytes 1769480 | tf_op jit(solution)/shard_map/ppermute | solution.py:415
  94.9 2.5 %shard_map.116.own = f32[384,768]{1,0:T(8,128)S(1)} custom-call(s32[16]{0:T(128)S(1)} %dynamic-slice_bitcast_fusion.table, f32[8,8]{1,0:T(8,128)S(1)} %copy-done.4, s32[8,8]{1,0:T(8,128)S(1)} %copy-done.5, f32[384,384]{1,0:T(8,128)S(1)} %get-tuple-element.37.x0, f32[384,384]{1,0:T(8,128)S(1)} %get-tuple-element.38.x1, ...), custom_call_target="tpu_custom_call" | custom-call | tf_op jit(solution)/shard_map/pallas_call | solution.py:375
  97.4 8.0 %collective-permute-done.9.r1 = f32[384,384]{1,0:T(8,128)S(1)} collective-permute-done((f32[384,384]{1,0:T(8,128)S(1)}, f32[384,384]{1,0:T(8,128)S(1)}, u32[]{:S(2)}, u32[]{:S(2)}) %collective-permute-start.9) | collective-permute-done | bytes 589856 | tf_op jit(solution)/shard_map/ppermute | solution.py:415
  105.4 3.8 %collective-permute-done.11.r3 = f32[384,384]{1,0:T(8,128)S(1)} collective-permute-done((f32[384,384]{1,0:T(8,128)S(1)}, f32[384,384]{1,0:T(8,128)S(1)}, u32[]{:S(2)}, u32[]{:S(2)}) %collective-permute-start.11) | collective-permute-done | bytes 589856 | tf_op jit(solution)/shard_map/ppermute | solution.py:415
  109.3 3.8 %shard_map.117 = (f32[384,384]{1,0:T(8,128)S(1)}, f32[384,384]{1,0:T(8,128)S(1)}) custom-call(s32[16]{0:T(128)S(1)} %dynamic-slice_bitcast_fusion.table, f32[8,8]{1,0:T(8,128)S(1)} %copy-done.4, s32[8,8]{1,0:T(8,128)S(1)} %copy-done.5, f32[384,384]{1,0:T(8,128)S(1)} %get-tuple-element.37.x0, f32[384,384]{1,0:T(8,128)S(1)} %get-tuple-element.38.x1, ...), custom_call_target="tpu_custom_call" | custom-call | tf_op jit(solution)/shard_map/pallas_call | solution.py:399
  113.1 3.3 %collective-permute-start.12 = (f32[384,384]{1,0:T(8,128)S(1)}, f32[384,384]{1,0:T(8,128)S(1)}, u32[]{:S(2)}, u32[]{:S(2)}) collective-permute-start(f32[384,384]{1,0:T(8,128)S(1)} %get-tuple-element.39), channel_id=1, source_target_pairs={{5,4},{1,1},{7,12},{6,2},{3,20},{10,3},{15,28},{13,8},{14,5},{2,16... | collective-permute-start | bytes 1769480 | tf_op jit(solution)/shard_map/ppermute | solution.py:447
  116.5 6.5 %collective-permute-start.13 = (f32[384,384]{1,0:T(8,128)S(1)}, f32[384,384]{1,0:T(8,128)S(1)}, u32[]{:S(2)}, u32[]{:S(2)}) collective-permute-start(f32[384,384]{1,0:T(8,128)S(1)} %get-tuple-element.40), channel_id=1, source_target_pairs={{5,0},{1,8},{7,1},{6,16},{3,2},{10,24},{15,3},{13,5},{14,12},{2,6}... | collective-permute-start | bytes 1769480 | tf_op jit(solution)/shard_map/ppermute | solution.py:447
  123.0 11.8 %collective-permute-done.12 = f32[384,384]{1,0:T(8,128)S(1)} collective-permute-done((f32[384,384]{1,0:T(8,128)S(1)}, f32[384,384]{1,0:T(8,128)S(1)}, u32[]{:S(2)}, u32[]{:S(2)}) %collective-permute-start.12) | collective-permute-done | bytes 589856 | tf_op jit(solution)/shard_map/ppermute | solution.py:447
  134.8 2.8 %collective-permute-done.13 = f32[384,384]{1,0:T(8,128)S(1)} collective-permute-done((f32[384,384]{1,0:T(8,128)S(1)}, f32[384,384]{1,0:T(8,128)S(1)}, u32[]{:S(2)}, u32[]{:S(2)}) %collective-permute-start.13) | collective-permute-done | bytes 589856 | tf_op jit(solution)/shard_map/ppermute | solution.py:447
  137.6 1.1 maximum_bitcast_fusion
  (30 shorter events, 2.0 us)
Async XLA Ops:
  0.0 1.3 copy-start
  2.2 1.3 copy-start.1
  2.2 1.3 copy-start.8
  2.3 18.4 %copy-start.9 = (f32[384]{0:T(512)S(1)}, f32[384]{0:T(512)}, u32[]{:S(2)}) copy-start(f32[384]{0:T(512)} %param.16) | copy-start | bytes 4612
  2.3 18.5 %copy-start.4 = (f32[8,8]{1,0:T(8,128)S(1)}, f32[8,8]{1,0:T(8,128)}, u32[]{:S(2)}) copy-start(f32[8,8]{1,0:T(8,128)} %occ.9) | copy-start | bytes 772
  3.5 18.1 %copy-start.6 = (s32[3,3]{1,0:T(4,128)S(1)}, s32[3,3]{1,0:T(4,128)}, u32[]{:S(2)}) copy-start(s32[3,3]{1,0:T(4,128)} %fock_tiles.1) | copy-start | bytes 112
  3.5 18.1 %copy-start.7 = (s32[3,3]{1,0:T(4,128)S(1)}, s32[3,3]{1,0:T(4,128)}, u32[]{:S(2)}) copy-start(s32[3,3]{1,0:T(4,128)} %over_tiles.1) | copy-start | bytes 112
  5.4 62.3 %collective-permute-start.6 = (f32[392,384]{1,0:T(8,128)}, f32[392,384]{1,0:T(8,128)S(1)}, u32[]{:S(2)}, u32[]{:S(2)}) collective-permute-start(f32[392,384]{1,0:T(8,128)} %get-tuple-element.35), channel_id=1, source_target_pairs={{4,5},{1,1},{12,7},{2,6},{20,3},{3,10},{28,15},{8,13},{5,14},{16,2... | collective-permute-start | bytes 1806344 | tf_op jit(solution)/shard_map/ppermute | solution.py:415
  10.3 15.4 %collective-permute-start = (f32[384,384]{1,0:T(8,128)}, f32[384,384]{1,0:T(8,128)S(1)}, u32[]{:S(2)}, u32[]{:S(2)}) collective-permute-start(f32[384,384]{1,0:T(8,128)} %shard_map.109), channel_id=1, source_target_pairs={{4,5},{1,1},{12,7},{2,6},{20,3},{3,10},{28,15},{8,13},{5,14},{16,2... | collective-permute-start | bytes 1769480 | tf_op jit(solution)/shard_map/ppermute | solution.py:415
  12.2 53.5 %collective-permute-start.1 = (f32[384,384]{1,0:T(8,128)S(1)}, f32[384,384]{1,0:T(8,128)S(1)}, u32[]{:S(2)}, u32[]{:S(2)}) collective-permute-start(f32[384,384]{1,0:T(8,128)S(1)} %shard_map.112), channel_id=1, source_target_pairs={{0,5},{8,1},{1,7},{16,6},{2,3},{24,10},{3,15},{5,13},{12,14},{6,2}... | collective-permute-start | bytes 1769480 | tf_op jit(solution)/shard_map/ppermute | solution.py:415
  17.9 55.8 %collective-permute-start.7 = (f32[392,384]{1,0:T(8,128)}, f32[392,384]{1,0:T(8,128)S(1)}, u32[]{:S(2)}, u32[]{:S(2)}) collective-permute-start(f32[392,384]{1,0:T(8,128)} %get-tuple-element.36), channel_id=1, source_target_pairs={{0,5},{8,1},{1,7},{16,6},{2,3},{24,10},{3,15},{5,13},{12,14},{6,2}... | collective-permute-start | bytes 1806344 | tf_op jit(solution)/shard_map/ppermute | solution.py:415
  19.9 1.8 %copy-start.2 = (f32[384,384]{1,0:T(8,128)S(1)}, f32[384,384]{1,0:T(8,128)}, u32[]{:S(2)}) copy-start(f32[384,384]{1,0:T(8,128)} %fock.1) | copy-start | bytes 1769476
  19.9 1.8 %copy-start.3 = (f32[384,384]{1,0:T(8,128)S(1)}, f32[384,384]{1,0:T(8,128)}, u32[]{:S(2)}) copy-start(f32[384,384]{1,0:T(8,128)} %over.1) | copy-start | bytes 1769476
  20.8 48.7 %copy-start.5 = (s32[8,8]{1,0:T(8,128)S(1)}, s32[8,8]{1,0:T(8,128)}, u32[]{:S(2)}) copy-start(s32[8,8]{1,0:T(8,128)} %pattern.7) | copy-start | bytes 772
  25.7 56.9 %collective-permute-start.3 = (f32[384,384]{1,0:T(8,128)S(1)}, f32[384,384]{1,0:T(8,128)S(1)}, u32[]{:S(2)}, u32[]{:S(2)}) collective-permute-start(f32[384,384]{1,0:T(8,128)S(1)} %collective-permute-done.x0), channel_id=1, source_target_pairs={{5,1},{14,11},{0,17},{12,28},{13,4},{9,13},{19,2},{16,8},{7,6},{11... | collective-permute-start | bytes 1769480 | tf_op jit(solution)/shard_map/ppermute | solution.py:415
  65.7 15.0 %collective-permute-start.5 = (f32[384,384]{1,0:T(8,128)S(1)}, f32[384,384]{1,0:T(8,128)S(1)}, u32[]{:S(2)}, u32[]{:S(2)}) collective-permute-start(f32[384,384]{1,0:T(8,128)S(1)} %collective-permute-done.1.x1), channel_id=1, source_target_pairs={{4,13},{13,9},{2,19},{8,16},{1,5},{11,14},{17,0},{28,12},{14,2},{9... | collective-permute-start | bytes 1769480 | tf_op jit(solution)/shard_map/ppermute | solution.py:415
  67.7 15.0 %collective-permute-start.4 = (f32[384,384]{1,0:T(8,128)S(1)}, f32[384,384]{1,0:T(8,128)S(1)}, u32[]{:S(2)}, u32[]{:S(2)}) collective-permute-start(f32[384,384]{1,0:T(8,128)S(1)} %collective-permute-done.1.x1), channel_id=1, source_target_pairs={{5,4},{7,14},{3,0},{15,12},{4,5},{13,1},{2,6},{8,10},{1,7},{11,9},... | collective-permute-start | bytes 1769480 | tf_op jit(solution)/shard_map/ppermute | solution.py:415
  67.7 15.6 %collective-permute-start.2 = (f32[384,384]{1,0:T(8,128)S(1)}, f32[384,384]{1,0:T(8,128)S(1)}, u32[]{:S(2)}, u32[]{:S(2)}) collective-permute-start(f32[384,384]{1,0:T(8,128)S(1)} %collective-permute-done.x0), channel_id=1, source_target_pairs={{4,5},{1,13},{6,2},{10,8},{5,4},{14,7},{0,3},{12,15},{13,14},{9,11... | collective-permute-start | bytes 1769480 | tf_op jit(solution)/shard_map/ppermute | solution.py:415
  87.3 18.1 %collective-permute-start.9 = (f32[384,384]{1,0:T(8,128)S(1)}, f32[384,384]{1,0:T(8,128)S(1)}, u32[]{:S(2)}, u32[]{:S(2)}) collective-permute-start(f32[384,384]{1,0:T(8,128)S(1)} %get-tuple-element.37.x0), channel_id=1, source_target_pairs={{5,1},{14,11},{0,17},{12,28},{13,4},{9,13},{19,2},{16,8},{7,6},{11... | collective-permute-start | bytes 1769480 | tf_op jit(solution)/shard_map/ppermute | solution.py:415
  89.2 16.2 %collective-permute-start.8 = (f32[384,384]{1,0:T(8,128)S(1)}, f32[384,384]{1,0:T(8,128)S(1)}, u32[]{:S(2)}, u32[]{:S(2)}) collective-permute-start(f32[384,384]{1,0:T(8,128)S(1)} %get-tuple-element.37.x0), channel_id=1, source_target_pairs={{4,5},{1,13},{6,2},{10,8},{5,4},{14,7},{0,3},{12,15},{13,14},{9,11... | collective-permute-start | bytes 1769480 | tf_op jit(solution)/shard_map/ppermute | solution.py:415
  89.3 19.9 %collective-permute-start.11 = (f32[384,384]{1,0:T(8,128)S(1)}, f32[384,384]{1,0:T(8,128)S(1)}, u32[]{:S(2)}, u32[]{:S(2)}) collective-permute-start(f32[384,384]{1,0:T(8,128)S(1)} %get-tuple-element.38.x1), channel_id=1, source_target_pairs={{4,13},{13,9},{2,19},{8,16},{1,5},{11,14},{17,0},{28,12},{14,2},{9... | collective-permute-start | bytes 1769480 | tf_op jit(solution)/shard_map/ppermute | solution.py:415
  93.2 16.1 %collective-permute-start.10 = (f32[384,384]{1,0:T(8,128)S(1)}, f32[384,384]{1,0:T(8,128)S(1)}, u32[]{:S(2)}, u32[]{:S(2)}) collective-permute-start(f32[384,384]{1,0:T(8,128)S(1)} %get-tuple-element.38.x1), channel_id=1, source_target_pairs={{5,4},{7,14},{3,0},{15,12},{4,5},{13,1},{2,6},{8,10},{1,7},{11,9},... | collective-permute-start | bytes 1769480 | tf_op jit(solution)/shard_map/ppermute | solution.py:415
  113.1 21.7 %collective-permute-start.12 = (f32[384,384]{1,0:T(8,128)S(1)}, f32[384,384]{1,0:T(8,128)S(1)}, u32[]{:S(2)}, u32[]{:S(2)}) collective-permute-start(f32[384,384]{1,0:T(8,128)S(1)} %get-tuple-element.39), channel_id=1, source_target_pairs={{5,4},{1,1},{7,12},{6,2},{3,20},{10,3},{15,28},{13,8},{14,5},{2,16... | collective-permute-start | bytes 1769480 | tf_op jit(solution)/shard_map/ppermute | solution.py:447
  116.5 21.1 %collective-permute-start.13 = (f32[384,384]{1,0:T(8,128)S(1)}, f32[384,384]{1,0:T(8,128)S(1)}, u32[]{:S(2)}, u32[]{:S(2)}) collective-permute-start(f32[384,384]{1,0:T(8,128)S(1)} %get-tuple-element.40), channel_id=1, source_target_pairs={{5,0},{1,8},{7,1},{6,16},{3,2},{10,24},{15,3},{13,5},{14,12},{2,6}... | collective-permute-start | bytes 1769480 | tf_op jit(solution)/shard_map/ppermute | solution.py:447
where the time goes:
time: 141 us; the launch traced here: 139 us
  waiting for transfers between devices  78.1 us (55%)
  starting transfers between devices  38.3 us (27%)
  Pallas kernels  17.5 us (12%)
  local copies, waits for them, and re-layouts  3.28 us (2%)
    ppermute x12, waiting for transfers between devices, send(): value = lax.ppermute(value, AXES, moves)  63.6 us
    ppermute x12, starting transfers between devices, send(): value = lax.ppermute(value, AXES, moves)  28.5 us
    ppermute x2, waiting for transfers between devices, shards(): lax.ppermute(value, AXES, [(target, source) for source, target in moves])  14.5 us
    ppermute x2, starting transfers between devices, shards(): lax.ppermute(value, AXES, [(target, source) for source, target in moves])  9.84 us
    pallas_call x2, Pallas kernels, update(): pl.pallas_call(update_kernel, compiler_params=LIMIT, in_specs=[SMEM()] *...  7.75 us
    pallas_call x2, Pallas kernels, own_part(): pl.pallas_call(own_kernel, compiler_params=LIMIT, in_specs=[SMEM()] * 3 +...  5.02 us
  transfers between devices with their start and end apart: 14, of which 11 were waited for; matrix products, arithmetic and copies ran while one was open for 1% of the time, Pallas kernels for 5%

commit v1 on v0

--- a/solution.py
+++ b/solution.py
@@ -119,7 +119,16 @@
         current[take], cost[take] = trial[take], trial_cost[take]
         if cost.min() < best_cost:
             best_cost, best = cost.min(), current[cost.argmin()].copy()
-    return [int(h) for h in best]
+    hosts = [int(h) for h in best]
+    owners = [[i * cols + j // 2 for i, j in unit] for unit in units]
+    for a in range(len(units)):
+        for b in range(a):
+            if chip_of_device[hosts[a]] == chip_of_device[hosts[b]]:
+                kept = owners[a].count(hosts[a]) + owners[b].count(hosts[b])
+                swapped = owners[a].count(hosts[b]) + owners[b].count(hosts[a])
+                if swapped < kept:
+                    hosts[a], hosts[b] = hosts[b], hosts[a]
+    return hosts
 
 
 def two_colours(edges):

time: 141 us -> 139 us (0.986); the launches traced: 139 us -> 138 us
  waiting for transfers between devices: 78.1 us -> 58.1 us
  starting transfers between devices: 38.3 us -> 58 us
    ppermute x12, starting transfers between devices: 28.5 us -> 54.9 us  [send(): value = lax.ppermute(value, AXES, moves)]
    ppermute x12, waiting for transfers between devices: 63.6 us -> 38.7 us  [send(): value = lax.ppermute(value, AXES, moves)]
    ppermute x2, starting transfers between devices: 9.84 us -> 3.16 us  [shards(): lax.ppermute(value, AXES, [(target, source) for source, target in moves])]
    ppermute x2, waiting for transfers between devices: 14.5 us -> 19.4 us  [shards(): lax.ppermute(value, AXES, [(target, source) for source, target in moves])]
  transfers between devices with their start and end apart: 14 -> 14, of which waited for: 11 -> 6; matrix products, arithmetic and copies ran while one was open for 1% -> 1% of each run, Pallas kernels for 5% -> 5%
where the time goes in v1:
time: 139 us; the launch traced here: 138 us
  waiting for transfers between devices  58.1 us (42%)
  starting transfers between devices  58 us (42%)
  Pallas kernels  17.5 us (13%)
  local copies, waits for them, and re-layouts  3.28 us (2%)
    ppermute x12, starting transfers between devices, send(): value = lax.ppermute(value, AXES, moves)  54.9 us
    ppermute x12, waiting for transfers between devices, send(): value = lax.ppermute(value, AXES, moves)  38.7 us
    ppermute x2, waiting for transfers between devices, shards(): lax.ppermute(value, AXES, [(target, source) for source, target in moves])  19.4 us
    pallas_call x2, Pallas kernels, update(): pl.pallas_call(update_kernel, compiler_params=LIMIT, in_specs=[SMEM()] *...  7.76 us
    pallas_call x2, Pallas kernels, own_part(): pl.pallas_call(own_kernel, compiler_params=LIMIT, in_specs=[SMEM()] * 3 +...  5.02 us
    ppermute x2, starting transfers between devices, shards(): lax.ppermute(value, AXES, [(target, source) for source, target in moves])  3.16 us
  transfers between devices with their start and end apart: 14, of which 6 were waited for; matrix products, arithmetic and copies ran while one was open for 1% of the time, Pallas kernels for 5%

profile of v1, /device:TPU:0, one launch (start us, length us, event | category | flops | bytes accessed | tf_op | source)
XLA Modules:
  0.0 138.5 jit_solution(5609117542125029163)
XLA Ops:
  0.0 1.3 copy-done
  1.3 1.0 shard_map.109
  2.3 0.1 shard_map.112
  2.4 1.1 copy-done.1
  3.5 1.9 %shard_map.114 = (f32[392,384]{1,0:T(8,128)}, f32[392,384]{1,0:T(8,128)}) custom-call(s32[2,3]{1,0:T(2,128)S(1)} %bitcast.15, f32[2,384,384]{2,1,0:T(8,128)S(1)} %bitcast.14), custom_call_target="tpu_custom_call" | custom-call | tf_op jit(solution)/shard_map/pallas_call | solution.py:372
  5.4 3.1 %collective-permute-start.6 = (f32[392,384]{1,0:T(8,128)}, f32[392,384]{1,0:T(8,128)S(1)}, u32[]{:S(2)}, u32[]{:S(2)}) collective-permute-start(f32[392,384]{1,0:T(8,128)} %get-tuple-element.35), channel_id=1, source_target_pairs={{4,5},{1,0},{12,7},{2,6},{20,3},{3,10},{28,15},{8,13},{5,14},{16,2... | collective-permute-start | bytes 1806344 | tf_op jit(solution)/shard_map/ppermute | solution.py:424
  8.5 0.1 collective-permute-start
  8.5 5.6 %collective-permute-start.1 = (f32[384,384]{1,0:T(8,128)S(1)}, f32[384,384]{1,0:T(8,128)S(1)}, u32[]{:S(2)}, u32[]{:S(2)}) collective-permute-start(f32[384,384]{1,0:T(8,128)S(1)} %shard_map.112), channel_id=1, source_target_pairs={{0,5},{8,0},{1,7},{16,6},{2,3},{24,10},{3,15},{5,13},{12,14},{6,2}... | collective-permute-start | bytes 1769480 | tf_op jit(solution)/shard_map/ppermute | solution.py:424
  14.1 1.9 %collective-permute-start.7 = (f32[392,384]{1,0:T(8,128)}, f32[392,384]{1,0:T(8,128)S(1)}, u32[]{:S(2)}, u32[]{:S(2)}) collective-permute-start(f32[392,384]{1,0:T(8,128)} %get-tuple-element.36), channel_id=1, source_target_pairs={{0,5},{8,0},{1,7},{16,6},{2,3},{24,10},{3,15},{5,13},{12,14},{6,2}... | collective-permute-start | bytes 1806344 | tf_op jit(solution)/shard_map/ppermute | solution.py:424
  16.1 0.8 dynamic-slice_bitcast_fusion.table
  16.9 0.1 broadcast_in_dim.12.e_col
  17.0 0.8 shard_map.111.scale
  17.9 0.9 shard_map.110
  18.9 3.8 %collective-permute-done.x0 = f32[384,384]{1,0:T(8,128)S(1)} collective-permute-done((f32[384,384]{1,0:T(8,128)}, f32[384,384]{1,0:T(8,128)S(1)}, u32[]{:S(2)}, u32[]{:S(2)}) %collective-permute-start) | collective-permute-done | bytes 589856 | tf_op jit(solution)/shard_map/ppermute | solution.py:424
  22.6 1.3 collective-permute-start.3
  23.9 4.9 %collective-permute-done.1.x1 = f32[384,384]{1,0:T(8,128)S(1)} collective-permute-done((f32[384,384]{1,0:T(8,128)S(1)}, f32[384,384]{1,0:T(8,128)S(1)}, u32[]{:S(2)}, u32[]{:S(2)}) %collective-permute-start.1) | collective-permute-done | bytes 589856 | tf_op jit(solution)/shard_map/ppermute | solution.py:424
  28.8 16.4 %collective-permute-start.5 = (f32[384,384]{1,0:T(8,128)S(1)}, f32[384,384]{1,0:T(8,128)S(1)}, u32[]{:S(2)}, u32[]{:S(2)}) collective-permute-start(f32[384,384]{1,0:T(8,128)S(1)} %collective-permute-done.1.x1), channel_id=1, source_target_pairs={{4,13},{13,8},{2,19},{9,16},{0,5},{11,14},{17,1},{28,12},{14,2},{8... | collective-permute-start | bytes 1769480 | tf_op jit(solution)/shard_map/ppermute | solution.py:424
  45.3 20.7 %collective-permute-start.2 = (f32[384,384]{1,0:T(8,128)S(1)}, f32[384,384]{1,0:T(8,128)S(1)}, u32[]{:S(2)}, u32[]{:S(2)}) collective-permute-start(f32[384,384]{1,0:T(8,128)S(1)} %collective-permute-done.x0), channel_id=1, source_target_pairs={{4,5},{0,13},{6,2},{10,9},{5,4},{14,7},{1,3},{12,15},{13,14},{8,11... | collective-permute-start | bytes 1769480 | tf_op jit(solution)/shard_map/ppermute | solution.py:424
  66.1 2.5 %shard_map.113.own = f32[384,768]{1,0:T(8,128)S(1)} custom-call(s32[16]{0:T(128)S(1)} %dynamic-slice_bitcast_fusion.table, f32[8,8]{1,0:T(8,128)S(1)} %copy-done.4, s32[8,8]{1,0:T(8,128)S(1)} %copy-done.5, f32[384,384]{1,0:T(8,128)S(1)} %collective-permute-done.x0, f32[384,384]{1,0:T(8,128)S(1)} %collective-permute-done.1.x1, ...), custom_call_target="tpu_custom_call" | custom-call | tf_op jit(solution)/shard_map/pallas_call | solution.py:384
  68.6 14.5 %collective-permute-done.4.r2 = f32[384,384]{1,0:T(8,128)S(1)} collective-permute-done((f32[384,384]{1,0:T(8,128)S(1)}, f32[384,384]{1,0:T(8,128)S(1)}, u32[]{:S(2)}, u32[]{:S(2)}) %collective-permute-start.4) | collective-permute-done | bytes 589856 | tf_op jit(solution)/shard_map/ppermute | solution.py:424
  83.1 3.9 %shard_map.115 = (f32[384,384]{1,0:T(8,128)S(1)}, f32[384,384]{1,0:T(8,128)S(1)}) custom-call(s32[16]{0:T(128)S(1)} %dynamic-slice_bitcast_fusion.table, f32[8,8]{1,0:T(8,128)S(1)} %copy-done.4, s32[8,8]{1,0:T(8,128)S(1)} %copy-done.5, f32[384,384]{1,0:T(8,128)S(1)} %collective-permute-done.x0, f32[384,384]{1,0:T(8,128)S(1)} %collective-permute-done.1.x1, ...), custom_call_target="tpu_custom_call" | custom-call | tf_op jit(solution)/shard_map/pallas_call | solution.py:408
  87.0 1.3 collective-permute-start.9
  88.4 4.3 %collective-permute-start.11 = (f32[384,384]{1,0:T(8,128)S(1)}, f32[384,384]{1,0:T(8,128)S(1)}, u32[]{:S(2)}, u32[]{:S(2)}) collective-permute-start(f32[384,384]{1,0:T(8,128)S(1)} %get-tuple-element.38.x1), channel_id=1, source_target_pairs={{4,13},{13,8},{2,19},{9,16},{0,5},{11,14},{17,1},{28,12},{14,2},{8... | collective-permute-start | bytes 1769480 | tf_op jit(solution)/shard_map/ppermute | solution.py:424
  92.8 2.5 %shard_map.116.own = f32[384,768]{1,0:T(8,128)S(1)} custom-call(s32[16]{0:T(128)S(1)} %dynamic-slice_bitcast_fusion.table, f32[8,8]{1,0:T(8,128)S(1)} %copy-done.4, s32[8,8]{1,0:T(8,128)S(1)} %copy-done.5, f32[384,384]{1,0:T(8,128)S(1)} %get-tuple-element.37.x0, f32[384,384]{1,0:T(8,128)S(1)} %get-tuple-element.38.x1, ...), custom_call_target="tpu_custom_call" | custom-call | tf_op jit(solution)/shard_map/pallas_call | solution.py:384
  95.3 15.6 %collective-permute-done.9.r1 = f32[384,384]{1,0:T(8,128)S(1)} collective-permute-done((f32[384,384]{1,0:T(8,128)S(1)}, f32[384,384]{1,0:T(8,128)S(1)}, u32[]{:S(2)}, u32[]{:S(2)}) %collective-permute-start.9) | collective-permute-done | bytes 589856 | tf_op jit(solution)/shard_map/ppermute | solution.py:424
  110.9 3.8 %shard_map.117 = (f32[384,384]{1,0:T(8,128)S(1)}, f32[384,384]{1,0:T(8,128)S(1)}) custom-call(s32[16]{0:T(128)S(1)} %dynamic-slice_bitcast_fusion.table, f32[8,8]{1,0:T(8,128)S(1)} %copy-done.4, s32[8,8]{1,0:T(8,128)S(1)} %copy-done.5, f32[384,384]{1,0:T(8,128)S(1)} %get-tuple-element.37.x0, f32[384,384]{1,0:T(8,128)S(1)} %get-tuple-element.38.x1, ...), custom_call_target="tpu_custom_call" | custom-call | tf_op jit(solution)/shard_map/pallas_call | solution.py:408
  114.7 0.1 collective-permute-start.12
  114.8 3.1 %collective-permute-start.13 = (f32[384,384]{1,0:T(8,128)S(1)}, f32[384,384]{1,0:T(8,128)S(1)}, u32[]{:S(2)}, u32[]{:S(2)}) collective-permute-start(f32[384,384]{1,0:T(8,128)S(1)} %get-tuple-element.40), channel_id=1, source_target_pairs={{5,0},{0,8},{7,1},{6,16},{3,2},{10,24},{15,3},{13,5},{14,12},{2,6}... | collective-permute-start | bytes 1769480 | tf_op jit(solution)/shard_map/ppermute | solution.py:456
  117.9 18.1 %collective-permute-done.12 = f32[384,384]{1,0:T(8,128)S(1)} collective-permute-done((f32[384,384]{1,0:T(8,128)S(1)}, f32[384,384]{1,0:T(8,128)S(1)}, u32[]{:S(2)}, u32[]{:S(2)}) %collective-permute-start.12) | collective-permute-done | bytes 589856 | tf_op jit(solution)/shard_map/ppermute | solution.py:456
  136.0 1.3 collective-permute-done.13
  137.3 0.1 select_bitcast_fusion.1
  137.4 1.1 maximum_bitcast_fusion
  (30 shorter events, 0.3 us)
Async XLA Ops:
  0.0 1.3 copy-start
  2.2 1.3 copy-start.1
  2.2 1.3 copy-start.8
  2.3 14.6 %copy-start.9 = (f32[384]{0:T(512)S(1)}, f32[384]{0:T(512)}, u32[]{:S(2)}) copy-start(f32[384]{0:T(512)} %param.16) | copy-start | bytes 4612
  2.3 14.7 %copy-start.4 = (f32[8,8]{1,0:T(8,128)S(1)}, f32[8,8]{1,0:T(8,128)}, u32[]{:S(2)}) copy-start(f32[8,8]{1,0:T(8,128)} %occ.9) | copy-start | bytes 772
  3.5 14.4 %copy-start.6 = (s32[3,3]{1,0:T(4,128)S(1)}, s32[3,3]{1,0:T(4,128)}, u32[]{:S(2)}) copy-start(s32[3,3]{1,0:T(4,128)} %fock_tiles.1) | copy-start | bytes 112
  3.5 14.4 %copy-start.7 = (s32[3,3]{1,0:T(4,128)S(1)}, s32[3,3]{1,0:T(4,128)}, u32[]{:S(2)}) copy-start(s32[3,3]{1,0:T(4,128)} %over_tiles.1) | copy-start | bytes 112
  5.4 39.9 %collective-permute-start.6 = (f32[392,384]{1,0:T(8,128)}, f32[392,384]{1,0:T(8,128)S(1)}, u32[]{:S(2)}, u32[]{:S(2)}) collective-permute-start(f32[392,384]{1,0:T(8,128)} %get-tuple-element.35), channel_id=1, source_target_pairs={{4,5},{1,0},{12,7},{2,6},{20,3},{3,10},{28,15},{8,13},{5,14},{16,2... | collective-permute-start | bytes 1806344 | tf_op jit(solution)/shard_map/ppermute | solution.py:424
  8.5 14.2 %collective-permute-start = (f32[384,384]{1,0:T(8,128)}, f32[384,384]{1,0:T(8,128)S(1)}, u32[]{:S(2)}, u32[]{:S(2)}) collective-permute-start(f32[384,384]{1,0:T(8,128)} %shard_map.109), channel_id=1, source_target_pairs={{4,5},{1,0},{12,7},{2,6},{20,3},{3,10},{28,15},{8,13},{5,14},{16,2... | collective-permute-start | bytes 1769480 | tf_op jit(solution)/shard_map/ppermute | solution.py:424
  8.5 20.3 %collective-permute-start.1 = (f32[384,384]{1,0:T(8,128)S(1)}, f32[384,384]{1,0:T(8,128)S(1)}, u32[]{:S(2)}, u32[]{:S(2)}) collective-permute-start(f32[384,384]{1,0:T(8,128)S(1)} %shard_map.112), channel_id=1, source_target_pairs={{0,5},{8,0},{1,7},{16,6},{2,3},{24,10},{3,15},{5,13},{12,14},{6,2}... | collective-permute-start | bytes 1769480 | tf_op jit(solution)/shard_map/ppermute | solution.py:424
  14.1 54.5 %collective-permute-start.7 = (f32[392,384]{1,0:T(8,128)}, f32[392,384]{1,0:T(8,128)S(1)}, u32[]{:S(2)}, u32[]{:S(2)}) collective-permute-start(f32[392,384]{1,0:T(8,128)} %get-tuple-element.36), channel_id=1, source_target_pairs={{0,5},{8,0},{1,7},{16,6},{2,3},{24,10},{3,15},{5,13},{12,14},{6,2}... | collective-permute-start | bytes 1806344 | tf_op jit(solution)/shard_map/ppermute | solution.py:424
  16.1 1.8 %copy-start.2 = (f32[384,384]{1,0:T(8,128)S(1)}, f32[384,384]{1,0:T(8,128)}, u32[]{:S(2)}) copy-start(f32[384,384]{1,0:T(8,128)} %fock.1) | copy-start | bytes 1769476
  16.1 1.8 %copy-start.3 = (f32[384,384]{1,0:T(8,128)S(1)}, f32[384,384]{1,0:T(8,128)}, u32[]{:S(2)}) copy-start(f32[384,384]{1,0:T(8,128)} %over.1) | copy-start | bytes 1769476
  17.0 49.1 %copy-start.5 = (s32[8,8]{1,0:T(8,128)S(1)}, s32[8,8]{1,0:T(8,128)}, u32[]{:S(2)}) copy-start(s32[8,8]{1,0:T(8,128)} %pattern.7) | copy-start | bytes 772
  22.6 60.4 %collective-permute-start.3 = (f32[384,384]{1,0:T(8,128)S(1)}, f32[384,384]{1,0:T(8,128)S(1)}, u32[]{:S(2)}, u32[]{:S(2)}) collective-permute-start(f32[384,384]{1,0:T(8,128)S(1)} %collective-permute-done.x0), channel_id=1, source_target_pairs={{5,0},{14,11},{1,17},{12,28},{13,4},{8,13},{19,2},{16,9},{7,6},{11... | collective-permute-start | bytes 1769480 | tf_op jit(solution)/shard_map/ppermute | solution.py:424
  28.8 39.8 %collective-permute-start.5 = (f32[384,384]{1,0:T(8,128)S(1)}, f32[384,384]{1,0:T(8,128)S(1)}, u32[]{:S(2)}, u32[]{:S(2)}) collective-permute-start(f32[384,384]{1,0:T(8,128)S(1)} %collective-permute-done.1.x1), channel_id=1, source_target_pairs={{4,13},{13,8},{2,19},{9,16},{0,5},{11,14},{17,1},{28,12},{14,2},{8... | collective-permute-start | bytes 1769480 | tf_op jit(solution)/shard_map/ppermute | solution.py:424
  45.2 37.8 %collective-permute-start.4 = (f32[384,384]{1,0:T(8,128)S(1)}, f32[384,384]{1,0:T(8,128)S(1)}, u32[]{:S(2)}, u32[]{:S(2)}) collective-permute-start(f32[384,384]{1,0:T(8,128)S(1)} %collective-permute-done.1.x1), channel_id=1, source_target_pairs={{5,4},{7,14},{3,1},{15,12},{4,5},{13,0},{2,6},{9,10},{0,7},{11,8},... | collective-permute-start | bytes 1769480 | tf_op jit(solution)/shard_map/ppermute | solution.py:424
  45.3 37.7 %collective-permute-start.2 = (f32[384,384]{1,0:T(8,128)S(1)}, f32[384,384]{1,0:T(8,128)S(1)}, u32[]{:S(2)}, u32[]{:S(2)}) collective-permute-start(f32[384,384]{1,0:T(8,128)S(1)} %collective-permute-done.x0), channel_id=1, source_target_pairs={{4,5},{0,13},{6,2},{10,9},{5,4},{14,7},{1,3},{12,15},{13,14},{8,11... | collective-permute-start | bytes 1769480 | tf_op jit(solution)/shard_map/ppermute | solution.py:424
  87.0 23.8 %collective-permute-start.9 = (f32[384,384]{1,0:T(8,128)S(1)}, f32[384,384]{1,0:T(8,128)S(1)}, u32[]{:S(2)}, u32[]{:S(2)}) collective-permute-start(f32[384,384]{1,0:T(8,128)S(1)} %get-tuple-element.37.x0), channel_id=1, source_target_pairs={{5,0},{14,11},{1,17},{12,28},{13,4},{8,13},{19,2},{16,9},{7,6},{11... | collective-permute-start | bytes 1769480 | tf_op jit(solution)/shard_map/ppermute | solution.py:424
  88.3 22.5 %collective-permute-start.8 = (f32[384,384]{1,0:T(8,128)S(1)}, f32[384,384]{1,0:T(8,128)S(1)}, u32[]{:S(2)}, u32[]{:S(2)}) collective-permute-start(f32[384,384]{1,0:T(8,128)S(1)} %get-tuple-element.37.x0), channel_id=1, source_target_pairs={{4,5},{0,13},{6,2},{10,9},{5,4},{14,7},{1,3},{12,15},{13,14},{8,11... | collective-permute-start | bytes 1769480 | tf_op jit(solution)/shard_map/ppermute | solution.py:424
  88.4 22.5 %collective-permute-start.11 = (f32[384,384]{1,0:T(8,128)S(1)}, f32[384,384]{1,0:T(8,128)S(1)}, u32[]{:S(2)}, u32[]{:S(2)}) collective-permute-start(f32[384,384]{1,0:T(8,128)S(1)} %get-tuple-element.38.x1), channel_id=1, source_target_pairs={{4,13},{13,8},{2,19},{9,16},{0,5},{11,14},{17,1},{28,12},{14,2},{8... | collective-permute-start | bytes 1769480 | tf_op jit(solution)/shard_map/ppermute | solution.py:424
  92.7 18.1 %collective-permute-start.10 = (f32[384,384]{1,0:T(8,128)S(1)}, f32[384,384]{1,0:T(8,128)S(1)}, u32[]{:S(2)}, u32[]{:S(2)}) collective-permute-start(f32[384,384]{1,0:T(8,128)S(1)} %get-tuple-element.38.x1), channel_id=1, source_target_pairs={{5,4},{7,14},{3,1},{15,12},{4,5},{13,0},{2,6},{9,10},{0,7},{11,8},... | collective-permute-start | bytes 1769480 | tf_op jit(solution)/shard_map/ppermute | solution.py:424
  114.7 21.3 %collective-permute-start.12 = (f32[384,384]{1,0:T(8,128)S(1)}, f32[384,384]{1,0:T(8,128)S(1)}, u32[]{:S(2)}, u32[]{:S(2)}) collective-permute-start(f32[384,384]{1,0:T(8,128)S(1)} %get-tuple-element.39), channel_id=1, source_target_pairs={{5,4},{0,1},{7,12},{6,2},{3,20},{10,3},{15,28},{13,8},{14,5},{2,16... | collective-permute-start | bytes 1769480 | tf_op jit(solution)/shard_map/ppermute | solution.py:456
  114.8 22.5 %collective-permute-start.13 = (f32[384,384]{1,0:T(8,128)S(1)}, f32[384,384]{1,0:T(8,128)S(1)}, u32[]{:S(2)}, u32[]{:S(2)}) collective-permute-start(f32[384,384]{1,0:T(8,128)S(1)} %get-tuple-element.40), channel_id=1, source_target_pairs={{5,0},{0,8},{7,1},{6,16},{3,2},{10,24},{15,3},{13,5},{14,12},{2,6}... | collective-permute-start | bytes 1769480 | tf_op jit(solution)/shard_map/ppermute | solution.py:456
